TPU v7x, 32 devices: a whole 2x2x4 slice. The times are simulated.
32 devices in a mesh: row: 8 (over z, y), col: 4 (over x, core).
Axes of the slice: x: 2, y: 2, z: 4, core: 2. Of those that a mesh axis runs over, the one named last changes fastest.
Arguments:
- sequence: bfloat16 [128, 1024], P('row'), may hold values from -6 to 6
- pair_state: bfloat16 [128, 128, 128], P('row', 'col'), may hold values from -6 to 6
- residue_mask: int32 [128], replicated, may hold values 0 or 1
- chain_index: int32 [128], replicated, may hold values from 0 to 3, never falling along the last dimension, each value on 1 to 64 neighbouring positions
- attention_in: bfloat16 [1024, 4, 1024], P(None, None, 'col'), may hold values from -0.1875 to 0.1875
- attention_out: bfloat16 [1024, 1024], P('col'), may hold values from -0.1875 to 0.1875
- bias_weight: bfloat16 [128, 32], replicated, may hold values from -40 to 40
- chain_bias: float32 [32], replicated, may hold values from -2 to 2
- outer_in: bfloat16 [1024, 128], replicated, may hold values from -0.1875 to 0.1875
- outer_out: bfloat16 [128, 128], replicated, may hold values from -0.5 to 0.5
- triangle_in: bfloat16 [128, 5, 128], replicated, may hold values from -0.5 to 0.5
- triangle_out: bfloat16 [128, 128], replicated, may hold values from -0.5 to 0.5
- transition_up: bfloat16 [128, 512], replicated, may hold values from -0.5 to 0.5
- transition_down: bfloat16 [512, 128], replicated, may hold values from -0.25 to 0.25
Outputs:
- sequence_out: bfloat16 [128, 1024], P('row')
- pair_out: bfloat16 [128, 128, 128], P('row', 'col')
Inputs may be any that keep to these rules, and one draw needn't show every extreme that they name: chain_index never falls along the residues; each chain holds at most 64 residues.
All inputs are finite; a program needn't handle non-finite values.
Results may differ from a plain program's by a relative error of at most 0.0095.
The roundings to bfloat16 on the way count: a program that leaves them out, or rounds other values in their place, can miss the bound.
Values may be sent and summed in bfloat16 or wider, within the bound.
A program may use at most 64 MiB of HBM per device.

v0:
```python
import math
import jax
import jax.numpy as jnp
from jax import lax
from jax.sharding import PartitionSpec as P


def layer_norm(values):
    center = values - jnp.mean(values, axis=-1, keepdims=True)
    spread = jnp.mean(center * center, axis=-1, keepdims=True)
    return center * lax.rsqrt(spread + 1e-05)


def per_device(
    sequence,
    pair_state,
    residue_mask,
    chain_index,
    attention_in,
    attention_out,
    bias_weight,
    chain_bias,
    outer_in,
    outer_out,
    triangle_in,
    triangle_out,
    transition_up,
    transition_down,
):
    rows_here, cols_here, channels = pair_state.shape
    length_all = residue_mask.shape[0]
    row_index = lax.axis_index("row")
    col_index = lax.axis_index("col")
    row_start = row_index * rows_here
    col_start = col_index * cols_here
    pair_wide = pair_state.astype(jnp.float32)
    normed_pair = layer_norm(pair_wide).astype(jnp.bfloat16)
    bias_tile = jnp.einsum(
        "ijc,ch->hij", normed_pair, bias_weight, preferred_element_type=jnp.float32
    )
    pair_bias = lax.all_to_all(bias_tile, "col", split_axis=0, concat_axis=2, tiled=True)
    heads_here = pair_bias.shape[0]
    normed_seq = layer_norm(sequence.astype(jnp.float32)).astype(jnp.bfloat16)
    projected = jnp.einsum(
        "id,dpe->ipe", normed_seq, attention_in, preferred_element_type=jnp.float32
    )
    query = projected[:, 0].astype(jnp.bfloat16)
    key_rows = projected[:, 1].astype(jnp.bfloat16)
    value_rows = projected[:, 2].astype(jnp.bfloat16)
    gate = jax.nn.sigmoid(projected[:, 3])
    keys_all, values_all = (
        lax.all_gather(key_rows, "row", axis=0, tiled=True),
        lax.all_gather(value_rows, "row", axis=0, tiled=True),
    )
    head_width = query.shape[1] // heads_here
    query_heads = query.reshape(rows_here, heads_here, head_width)
    key_heads = keys_all.reshape(length_all, heads_here, head_width)
    value_heads = values_all.reshape(length_all, heads_here, head_width)
    scale = 1.0 / math.sqrt(head_width)
    scores = (
        jnp.einsum("ihd,jhd->hij", query_heads, key_heads, preferred_element_type=jnp.float32)
        * scale
    )
    chain_rows = lax.dynamic_slice_in_dim(chain_index, row_start, rows_here, 0)
    same_chain = (chain_rows[:, None] == chain_index[None, :]).astype(jnp.float32)
    head_offset = lax.dynamic_slice_in_dim(chain_bias, col_index * heads_here, heads_here, 0)
    scores = scores + pair_bias + head_offset[:, None, None] * same_chain[None]
    positions = jnp.arange(length_all, dtype=jnp.int32)
    query_ids = row_start + jnp.arange(rows_here, dtype=jnp.int32)
    allowed = (residue_mask[None, :] == 1) | (query_ids[:, None] == positions[None, :])
    allowed = allowed[None]
    highest = jnp.max(jnp.where(allowed, scores, -jnp.inf), axis=-1, keepdims=True)
    raised = jnp.where(allowed, jnp.exp(scores - highest), 0.0)
    weights = (raised / jnp.sum(raised, axis=-1, keepdims=True)).astype(jnp.bfloat16)
    gathered = jnp.einsum(
        "hij,jhd->ihd", weights, value_heads, preferred_element_type=jnp.float32
    ).reshape(rows_here, -1)
    mixed = (gate * gathered).astype(jnp.bfloat16)
    head_terms = jnp.dot(mixed, attention_out, preferred_element_type=jnp.float32)
    update = lax.psum(head_terms, "col")
    sequence_out = (sequence.astype(jnp.float32) + update).astype(jnp.bfloat16)
    normed_out = layer_norm(sequence_out.astype(jnp.float32)).astype(jnp.bfloat16)
    outer_rows = jnp.dot(normed_out, outer_in, preferred_element_type=jnp.float32).astype(
        jnp.bfloat16
    )
    half_width = outer_rows.shape[1] // 2
    right_all = lax.all_gather(outer_rows[:, half_width:], "row", axis=0, tiled=True)
    right_side = lax.dynamic_slice_in_dim(right_all, col_start, cols_here, 0).astype(jnp.float32)
    left_side = outer_rows[:, :half_width].astype(jnp.float32)
    outer_feat = jnp.concatenate(
        [
            left_side[:, None, :] * right_side[None, :, :],
            left_side[:, None, :] - right_side[None, :, :],
        ],
        axis=-1,
    ).astype(jnp.bfloat16)
    pair_mid = pair_wide + jnp.dot(
        outer_feat.reshape(-1, 2 * half_width), outer_out, preferred_element_type=jnp.float32
    ).reshape(rows_here, cols_here, channels)
    normed_mid = layer_norm(pair_mid).astype(jnp.bfloat16)
    tri = jnp.dot(
        normed_mid.reshape(-1, channels),
        triangle_in.reshape(channels, -1),
        preferred_element_type=jnp.float32,
    ).reshape(rows_here, cols_here, 5, channels)
    live = residue_mask.astype(jnp.float32)
    row_live = lax.dynamic_slice_in_dim(live, row_start, rows_here, 0)
    col_live = lax.dynamic_slice_in_dim(live, col_start, cols_here, 0)
    pair_live = (row_live[:, None] * col_live[None, :])[:, :, None]
    left_op = (jax.nn.sigmoid(tri[:, :, 0]) * tri[:, :, 1] * pair_live).astype(jnp.bfloat16)
    right_op = (jax.nn.sigmoid(tri[:, :, 2]) * tri[:, :, 3] * pair_live).astype(jnp.bfloat16)
    out_gate = jax.nn.sigmoid(tri[:, :, 4])
    column_all = lax.all_gather(right_op, "row", axis=0, tiled=True)
    crossed = lax.psum_scatter(
        jnp.einsum("jkc,ikc->jic", column_all, left_op, preferred_element_type=jnp.float32),
        "col",
        scatter_dimension=0,
        tiled=True,
    )
    product = jnp.transpose(crossed, (1, 0, 2))
    normed_product = layer_norm(product).astype(jnp.bfloat16)
    projected_product = jnp.dot(
        normed_product.reshape(-1, channels), triangle_out, preferred_element_type=jnp.float32
    ).reshape(rows_here, cols_here, channels)
    pair_late = pair_mid + out_gate * projected_product
    normed_late = layer_norm(pair_late).astype(jnp.bfloat16)
    hidden = jax.nn.relu(
        jnp.dot(
            normed_late.reshape(-1, channels), transition_up, preferred_element_type=jnp.float32
        )
    ).astype(jnp.bfloat16)
    lowered = jnp.dot(hidden, transition_down, preferred_element_type=jnp.float32).reshape(
        rows_here, cols_here, channels
    )
    pair_out = (pair_late + lowered).astype(jnp.bfloat16)
    return (sequence_out, pair_out)


def solution(mesh):
    return jax.shard_map(
        per_device,
        mesh=mesh,
        in_specs=(
            P("row", None),
            P("row", "col", None),
            P(),
            P(),
            P(None, None, "col"),
            P("col", None),
            P(),
            P(),
            P(),
            P(),
            P(),
            P(),
            P(),
            P(),
        ),
        out_specs=(P("row", None), P("row", "col", None)),
        check_vma=False,
    )
```

profile of v0, /device:TPU:0, one launch (start us, length us, event | category | flops | bytes accessed | tf_op | source)
XLA Modules:
  0.0 257.6 jit_solution(43655018280628967)
XLA Ops:
  7.2 1.2 convert_reduce_fusion
  8.4 1.2 fusion.14
  9.6 1.2 convolution_bitcast_fusion.1
  10.8 0.2 copy.92
  11.0 0.8 reshape.259
  11.8 4.2 %all-to-all-start = ((f32[4,1,4096]{2,1,0:T(1,128)}), f32[4,1,4096]{2,1,0:T(1,128)S(1)}, u32[]{:S(2)}, u32[]{:S(2)}) async-start(f32[4,1,4096]{2,1,0:T(1,128)} %reshape.259), calls=%async_computation | async-start | bytes 131072 | tf_op jit(solution)/shard_map/all_to_all | solution.py:41
  16.0 0.7 convert_element_type.101
  16.7 0.7 broadcast_compare_fusion
  17.3 0.6 dynamic_slice.19
  17.9 0.7 dynamic_slice.18
  18.6 0.7 dynamic_slice.16
  19.3 0.9 convert_reduce_fusion.1
  20.2 0.9 fusion.50
  21.1 0.7 compare_convert_fusion
  21.9 1.9 fusion.92
  23.7 0.7 convert_element_type.87
  24.5 0.1 fusion.78
  24.5 31.5 %all-gather.1 = bf16[128,1,256]{2,0,1:T(8,128)(2,1)S(1)} all-gather(bf16[16,1,256]{2,0,1:T(8,128)(2,1)S(1)} %get-tuple-element.7), channel_id=3, replica_groups=mesh['row'=8,'col'=4] {'row'}, dimensions={0}, use_global_device_ids=true | all-gather | bytes 73728 | tf_op jit(solution)/shard_map/all_gather | solution.py:52
  56.0 0.1 copy.90
  56.1 30.5 %all-gather = bf16[128,1,256]{2,0,1:T(8,128)(2,1)S(1)} all-gather(bf16[16,1,256]{2,0,1:T(8,128)(2,1)S(1)} %get-tuple-element.8), channel_id=2, replica_groups=mesh['row'=8,'col'=4] {'row'}, dimensions={0}, use_global_device_ids=true | all-gather | bytes 73728 | tf_op jit(solution)/shard_map/all_gather | solution.py:53
  86.6 0.7 copy.89
  87.4 0.1 dynamic_slice.15
  87.4 0.5 broadcast.233
  88.0 0.8 reduce
  88.8 0.1 reshape.260
  88.9 0.2 copy.93
  89.1 0.2 all_to_all.16
  89.2 0.9 fusion.10
  90.2 0.2 fusion.93
  90.4 1.1 convolution_bitcast_fusion.2
  91.6 0.1 reshape.243
  91.6 1.5 fusion.74
  93.3 0.7 broadcast_multiply_fusion
  94.0 0.8 copy.95
  94.8 31.4 %all-reduce.2.cloned.1.call-done = f32[16,1024]{1,0:T(8,128)} async-done(((f32[16,1024]{1,0:T(8,128)}), f32[16,1024]{1,0:T(8,128)}) %all-reduce.2.cloned.1.call-update) | async-done | bytes 65552 | tf_op jit(solution)/shard_map/psum | solution.py:80
  126.2 1.0 convert_reduce_fusion.2
  127.2 0.2 fusion.52
  127.4 0.2 convolution_convert_fusion
  127.6 0.1 slice_convert_fusion
  127.7 30.7 %all_gather.14 = bf16[128,64]{1,0:T(8,128)(2,1)S(1)} all-gather(bf16[16,64]{1,0:T(8,128)(2,1)S(1)} %get-tuple-element.12), channel_id=1, replica_groups=mesh['row'=8,'col'=4] {'row'}, dimensions={0}, use_global_device_ids=true | all-gather | bytes 18432 | tf_op jit(solution)/shard_map/all_gather | solution.py:87
  158.4 1.1 fusion.94
  159.6 0.3 multiply_reduce_fusion.2
  159.8 0.4 copy-done.2
  160.3 1.3 fusion.32
  161.6 0.8 fusion.18
  162.5 1.2 copy.101
  163.7 39.1 %all-gather.4.cloned.1.call-done = bf16[128,32,128]{2,1,0:T(8,128)(2,1)} async-done(((bf16[16,32,128]{2,1,0:T(8,128)(2,1)}), bf16[128,32,128]{2,1,0:T(8,128)(2,1)}) %all-gather.4.cloned.1.call-update) | async-done | bytes 1048592 | tf_op jit(solution)/shard_map/all_gather | solution.py:113
  202.8 7.3 %copy.102 = bf16[128,32,128]{1,0,2:T(8,128)(2,1)} copy(bf16[128,32,128]{2,1,0:T(8,128)(2,1)} %all-gather.4.cloned.1.call-done) | data formatting | bytes 2097152 | tf_op jit(solution)/shard_map/all_gather | solution.py:113
  210.0 5.6 %convolution_bitcast_fusion = f32[128,16,128]{0,1,2:T(8,128)} fusion(bf16[16,32,128]{1,0,2:T(8,128)(2,1)} %copy.101, bf16[128,32,128]{1,0,2:T(8,128)(2,1)} %copy.102), kind=kOutput, calls=%fused_computation.4 | convolution fusion | flops 16777216 | bytes 2228224 | tf_op jit(solution)/shard_map/jkc,ikc->jic/dot_general | solution.py:115
  215.6 2.8 %copy.103 = f32[128,16,128]{2,1,0:T(8,128)} copy(f32[128,16,128]{0,1,2:T(8,128)} %convolution_bitcast_fusion) | data formatting | bytes 2097152 | tf_op jit(solution)/shard_map/jkc,ikc->jic/transpose | solution.py:115
  218.4 23.7 %reduce-scatter.2.cloned.1.call-done = f32[32,16,128]{2,1,0:T(8,128)} async-done(((f32[128,16,128]{2,1,0:T(8,128)}), f32[32,16,128]{2,1,0:T(8,128)}) %reduce-scatter.2.cloned.1.call-update) | async-done | bytes 262160 | tf_op jit(solution)/shard_map/reduce_scatter | solution.py:114
  242.1 1.1 bitcast_reduce_fusion
  243.2 0.1 copy.104
  243.3 0.1 copy.105
  243.4 1.2 multiply_reduce_fusion.1
  244.6 0.1 copy.106
  244.7 0.1 copy.107
  244.7 1.2 multiply_convert_fusion.1
  245.9 1.3 fusion.95
  247.2 0.3 multiply_reduce_fusion
  247.5 0.4 copy-done.1
  247.9 0.2 multiply_convert_fusion
  248.1 1.3 fusion.4
  249.4 1.6 add_convert_fusion
  (44 shorter events, 0.3 us)
Async XLA Ops:
  7.2 14.7 %copy-start = (bf16[1024,4,256]{2,1,0:T(4,128)(2,1)S(1)}, bf16[1024,4,256]{2,1,0:T(4,128)(2,1)}, u32[]{:S(2)}) copy-start(bf16[1024,4,256]{2,1,0:T(4,128)(2,1)} %param.18) | copy-start | bytes 6291460
  9.6 77.8 %copy-start.10 = (f32[32]{0:T(128)S(1)}, f32[32]{0:T(128)}, u32[]{:S(2)}) copy-start(f32[32]{0:T(128)} %param.21) | copy-start | bytes 388
  11.8 75.7 %all-to-all-start = ((f32[4,1,4096]{2,1,0:T(1,128)}), f32[4,1,4096]{2,1,0:T(1,128)S(1)}, u32[]{:S(2)}, u32[]{:S(2)}) async-start(f32[4,1,4096]{2,1,0:T(1,128)} %reshape.259), calls=%async_computation | async-start | bytes 131072 | tf_op jit(solution)/shard_map/all_to_all | solution.py:41
  16.0 110.2 %all-reduce.2.cloned.1.call-start = ((), (), s32[]{:S(2)}) async-start(), calls=%async_computation.2 | async-start | bytes 131072 | tf_op jit(solution)/shard_map/psum | solution.py:80
  21.9 69.8 %copy-start.5 = (bf16[256,1024]{1,0:T(8,128)(2,1)S(1)}, bf16[256,1024]{1,0:T(8,128)(2,1)}, u32[]{:S(2)}) copy-start(bf16[256,1024]{1,0:T(8,128)(2,1)} %param.19) | copy-start | bytes 1572868
  23.7 70.3 %copy-start.6 = (bf16[128,5,128]{2,0,1:T(8,128)(2,1)S(1)}, bf16[128,5,128]{2,0,1:T(8,128)(2,1)}, u32[]{:S(2)}) copy-start(bf16[128,5,128]{2,0,1:T(8,128)(2,1)} %param.24) | copy-start | bytes 491524
  23.7 102.5 %copy-start.4 = (bf16[16,1024]{1,0:T(8,128)(2,1)S(1)}, bf16[16,1024]{1,0:T(8,128)(2,1)}, u32[]{:S(2)}) copy-start(bf16[16,1024]{1,0:T(8,128)(2,1)} %param.14) | copy-start | bytes 98308
  87.4 71.1 %copy-start.3 = (bf16[16,32,128]{2,1,0:T(8,128)(2,1)S(1)}, bf16[16,32,128]{2,1,0:T(8,128)(2,1)}, u32[]{:S(2)}) copy-start(bf16[16,32,128]{2,1,0:T(8,128)(2,1)} %param.15) | copy-start | bytes 393220
  89.2 38.2 %copy-start.8 = (bf16[1024,128]{1,0:T(8,128)(2,1)S(1)}, bf16[1024,128]{1,0:T(8,128)(2,1)}, u32[]{:S(2)}) copy-start(bf16[1024,128]{1,0:T(8,128)(2,1)} %param.22) | copy-start | bytes 786436
  93.2 109.6 %all-gather.4.cloned.1.call-start = ((), (), s32[]{:S(2)}) async-start(), calls=%async_computation.3 | async-start | bytes 1179648 | tf_op jit(solution)/shard_map/all_gather | solution.py:113
  127.2 32.6 %copy-start.7 = (bf16[16,1024]{1,0:T(8,128)(2,1)}, bf16[16,1024]{1,0:T(8,128)(2,1)S(1)}, u32[]{:S(2)}) copy-start(bf16[16,1024]{1,0:T(8,128)(2,1)S(1)} %get-tuple-element.3) | copy-start | bytes 98308
  159.5 0.7 copy-start.2
  162.4 79.7 %reduce-scatter.2.cloned.1.call-start = ((), (), s32[]{:S(2)}) async-start(), calls=%async_computation.4 | async-start | bytes 1310720 | tf_op jit(solution)/shard_map/reduce_scatter | solution.py:114
  245.9 2.2 copy-start.9
  247.2 0.7 copy-start.1
Sparse Core Ops, SparseCore 0:
  93.3 32.8 all-reduce.1
  162.5 40.1 all-gather.3
  218.6 23.5 reduce-scatter.1
where the time goes:
time: 259 us; the launch traced here: 258 us
  waiting for transfers between devices  94.3 us (36%)
  blocking collectives  92.7 us (36%)
  local copies, waits for them, and re-layouts  18.8 us (7%)
  matrix products  17.5 us (7%)
  other arithmetic  16 us (6%)
  between operations  14 us (5%)
  starting transfers between devices  4.32 us (2%)
    all_gather x1, waiting for transfers between devices, per_device(): column_all = lax.all_gather(right_op, 'row', axis=0, tiled=True)  39.1 us
    all_gather x1, blocking collectives, per_device(): lax.all_gather(key_rows, 'row', axis=0, tiled=True)  31.5 us
    psum x1, waiting for transfers between devices, per_device(): update = lax.psum(head_terms, 'col')  31.4 us
    all_gather x1, blocking collectives, per_device(): lax.all_gather(outer_rows[:, half_width:], 'row', axis=0, tiled=True)  30.7 us
    all_gather x1, blocking collectives, per_device(): lax.all_gather(value_rows, 'row', axis=0, tiled=True)  30.5 us
    reduce_scatter x1, waiting for transfers between devices, per_device(): lax.psum_scatter(jnp.einsum('jkc,ikc->jic', column_all, left_op, preferre...  23.7 us
    all_gather x1, local copies, waits for them, and re-layouts, per_device(): column_all = lax.all_gather(right_op, 'row', axis=0, tiled=True)  7.25 us
    dot_general x1, matrix products, per_device(): jnp.einsum('jkc,ikc->jic', column_all, left_op, preferred_element_type=jn...  5.6 us
  transfers between devices with their start and end apart: 4, of which 3 were waited for; matrix products, arithmetic and copies ran while one was open for 5% of the time, Pallas kernels for 0%

commit v1 on v0

--- a/solution.py
+++ b/solution.py
@@ -3,6 +3,21 @@
 import jax.numpy as jnp
 from jax import lax
 from jax.sharding import PartitionSpec as P
+
+
+def work_around(x, axis, dim, make, out_dim):
+    ways, here, step = (lax.axis_size(axis), lax.axis_index(axis), x.shape[dim])
+    results = []
+    for far in range(ways):
+        arriving = (
+            lax.ppermute(x, axis, [(d, (d + 1) % ways) for d in range(ways)])
+            if far + 1 < ways
+            else x
+        )
+        results.append(make(x, (here - far) % ways * step))
+        x = arriving
+    line = jnp.concatenate(results[::-1], axis=out_dim)
+    return jnp.roll(line, (here + 1) * results[0].shape[out_dim], axis=out_dim)
 
 
 def layer_norm(values):
@@ -110,9 +125,16 @@
     left_op = (jax.nn.sigmoid(tri[:, :, 0]) * tri[:, :, 1] * pair_live).astype(jnp.bfloat16)
     right_op = (jax.nn.sigmoid(tri[:, :, 2]) * tri[:, :, 3] * pair_live).astype(jnp.bfloat16)
     out_gate = jax.nn.sigmoid(tri[:, :, 4])
-    column_all = lax.all_gather(right_op, "row", axis=0, tiled=True)
     crossed = lax.psum_scatter(
-        jnp.einsum("jkc,ikc->jic", column_all, left_op, preferred_element_type=jnp.float32),
+        work_around(
+            right_op,
+            "row",
+            0,
+            lambda own_block, offset: jnp.einsum(
+                "jkc,ikc->jic", own_block, left_op, preferred_element_type=jnp.float32
+            ),
+            0,
+        ),
         "col",
         scatter_dimension=0,
         tiled=True,

time: 259 us -> 274 us (1.058)
  local copies, waits for them, and re-layouts: 18.8 us -> 32.3 us
  matrix products: 17.5 us -> 22.1 us
  waiting for transfers between devices: 94.3 us -> 90.5 us
    all_gather x1 -> x0, waiting for transfers between devices: 39.1 us -> none  [per_device(): column_all = lax.all_gather(right_op, 'row', axis=0, tiled=True)]
    ppermute x0 -> x7, waiting for transfers between devices: none -> 37.6 us  [work_around(): lax.ppermute(x, axis, [(d, (d + 1) % ways) for d in range(ways)])]
    concatenate x0 -> x1, local copies, waits for them, and re-layouts: none -> 13.1 us  [work_around(): return jnp.roll(line, (here + 1) * results[0].shape[out_dim], axis=out_dim)]
    all_gather x1 -> x0, local copies, waits for them, and re-layouts: 7.25 us -> none  [per_device(): column_all = lax.all_gather(right_op, 'row', axis=0, tiled=True)]
    ppermute x0 -> x7, local copies, waits for them, and re-layouts: none -> 6.69 us  [work_around(): lax.ppermute(x, axis, [(d, (d + 1) % ways) for d in range(ways)])]
    dot_general x1 -> x8, matrix products: 5.6 us -> 11.1 us  [per_device(): jnp.einsum('jkc,ikc->jic', own_block, left_op, preferred_element_type=jnp...]
    dynamic_slice x0 -> x2, local copies, waits for them, and re-layouts: none -> 3.54 us  [work_around(): return jnp.roll(line, (here + 1) * results[0].shape[out_dim], axis=out_dim)]
    reduce_scatter x1, waiting for transfers between devices: 23.7 us -> 20.8 us  [per_device(): lax.psum_scatter(work_around(right_op, 'row', 0, lambda own_block, offset...]
  transfers between devices with their start and end apart: 4 -> 10, of which waited for: 3 -> 9; matrix products, arithmetic and copies ran while one was open for 5% -> 10% of each run, Pallas kernels for 0% -> 0%
where the time goes in v1:
time: 274 us; the launch traced here: 273 us
  blocking collectives  92.7 us (34%)
  waiting for transfers between devices  90.5 us (33%)
  local copies, waits for them, and re-layouts  32.3 us (12%)
  matrix products  22.1 us (8%)
  other arithmetic  15.1 us (6%)
  between operations  14.4 us (5%)
  starting transfers between devices  5.77 us (2%)
    ppermute x7, waiting for transfers between devices, work_around(): lax.ppermute(x, axis, [(d, (d + 1) % ways) for d in range(ways)])  37.6 us
    psum x1, waiting for transfers between devices, per_device(): update = lax.psum(head_terms, 'col')  32.1 us
    all_gather x1, blocking collectives, per_device(): lax.all_gather(key_rows, 'row', axis=0, tiled=True)  31.5 us
    all_gather x1, blocking collectives, per_device(): lax.all_gather(outer_rows[:, half_width:], 'row', axis=0, tiled=True)  30.7 us
    all_gather x1, blocking collectives, per_device(): lax.all_gather(value_rows, 'row', axis=0, tiled=True)  30.5 us
    reduce_scatter x1, waiting for transfers between devices, per_device(): lax.psum_scatter(work_around(right_op, 'row', 0, lambda own_block, offset...  20.8 us
    concatenate x1, local copies, waits for them, and re-layouts, work_around(): return jnp.roll(line, (here + 1) * results[0].shape[out_dim], axis=out_dim)  13.1 us
    dot_general x8, matrix products, per_device(): jnp.einsum('jkc,ikc->jic', own_block, left_op, preferred_element_type=jnp...  11.1 us
  transfers between devices with their start and end apart: 10, of which 9 were waited for; matrix products, arithmetic and copies ran while one was open for 10% of the time, Pallas kernels for 0%

profile of v1, /device:TPU:0, one launch (start us, length us, event | category | flops | bytes accessed | tf_op | source)
XLA Modules:
  0.0 272.8 jit_solution(12061918019307983538)
XLA Ops:
  7.2 1.2 convert_reduce_fusion
  8.4 1.2 fusion.14
  9.6 1.2 convolution_bitcast_fusion.8
  11.0 0.8 reshape.259
  11.8 4.2 %all-to-all-start = ((f32[4,1,4096]{2,1,0:T(1,128)}), f32[4,1,4096]{2,1,0:T(1,128)S(1)}, u32[]{:S(2)}, u32[]{:S(2)}) async-start(f32[4,1,4096]{2,1,0:T(1,128)} %reshape.259), calls=%async_computation | async-start | bytes 131072 | tf_op jit(solution)/shard_map/all_to_all | solution.py:56
  16.0 0.7 convert_element_type.101
  16.7 0.7 broadcast_compare_fusion
  17.3 0.6 dynamic_slice.23
  17.9 0.7 dynamic_slice.22
  18.6 0.7 dynamic_slice.20
  19.3 0.9 convert_reduce_fusion.1
  20.2 0.9 fusion.50
  21.1 0.7 compare_convert_fusion
  21.9 1.9 fusion.92
  23.7 0.7 convert_element_type.87
  24.5 31.5 %all-gather.1 = bf16[128,1,256]{2,0,1:T(8,128)(2,1)S(1)} all-gather(bf16[16,1,256]{2,0,1:T(8,128)(2,1)S(1)} %get-tuple-element.7), channel_id=3, replica_groups=mesh['row'=8,'col'=4] {'row'}, dimensions={0}, use_global_device_ids=true | all-gather | bytes 73728 | tf_op jit(solution)/shard_map/all_gather | solution.py:67
  56.1 30.5 %all-gather = bf16[128,1,256]{2,0,1:T(8,128)(2,1)S(1)} all-gather(bf16[16,1,256]{2,0,1:T(8,128)(2,1)S(1)} %get-tuple-element.8), channel_id=2, replica_groups=mesh['row'=8,'col'=4] {'row'}, dimensions={0}, use_global_device_ids=true | all-gather | bytes 73728 | tf_op jit(solution)/shard_map/all_gather | solution.py:68
  86.6 0.7 copy.145
  87.4 0.5 broadcast.234
  88.0 0.8 reduce
  89.3 0.9 fusion.10
  90.4 1.1 convolution_bitcast_fusion.9
  91.6 1.5 fusion.74
  93.2 0.7 broadcast_multiply_fusion
  94.1 32.1 %all-reduce.2.cloned.1.call-done = f32[16,1024]{1,0:T(8,128)} async-done(((f32[16,1024]{1,0:T(8,128)}), f32[16,1024]{1,0:T(8,128)}) %all-reduce.2.cloned.1.call-update) | async-done | bytes 65552 | tf_op jit(solution)/shard_map/psum | solution.py:95
  126.2 1.0 convert_reduce_fusion.2
  127.4 1.2 convolution_convert_fusion
  128.6 30.7 %all_gather.11 = bf16[128,64]{1,0:T(8,128)(2,1)S(1)} all-gather(bf16[16,64]{1,0:T(8,128)(2,1)S(1)} %get-tuple-element.12), channel_id=1, replica_groups=mesh['row'=8,'col'=4] {'row'}, dimensions={0}, use_global_device_ids=true | all-gather | bytes 18432 | tf_op jit(solution)/shard_map/all_gather | solution.py:102
  159.4 1.1 fusion.94
  161.2 1.0 copy-done.1
  162.2 0.8 fusion.18
  163.0 1.5 collective-permute-start
  165.0 1.3 copy.157
  166.3 1.4 convolution_bitcast_fusion
  167.7 3.2 %collective-permute-done = bf16[16,32,128]{2,1,0:T(8,128)(2,1)} collective-permute-done((bf16[16,32,128]{2,1,0:T(8,128)(2,1)S(1)}, bf16[16,32,128]{2,1,0:T(8,128)(2,1)}, u32[]{:S(2)}, u32[]{:S(2)}) %collective-permute-start) | collective-permute-done | bytes 131104 | tf_op jit(solution)/shard_map/ppermute | solution.py:13
  170.8 1.4 copy.170
  172.2 1.4 convolution_bitcast_fusion.1
  173.6 5.1 %collective-permute-done.1 = bf16[16,32,128]{2,1,0:T(8,128)(2,1)S(1)} collective-permute-done((bf16[16,32,128]{2,1,0:T(8,128)(2,1)}, bf16[16,32,128]{2,1,0:T(8,128)(2,1)S(1)}, u32[]{:S(2)}, u32[]{:S(2)}) %collective-permute-start.1) | collective-permute-done | bytes 131104 | tf_op jit(solution)/shard_map/ppermute | solution.py:13
  178.7 0.4 copy.168
  179.1 1.4 convolution_bitcast_fusion.2
  180.5 5.9 %collective-permute-done.2 = bf16[16,32,128]{2,1,0:T(8,128)(2,1)} collective-permute-done((bf16[16,32,128]{2,1,0:T(8,128)(2,1)S(1)}, bf16[16,32,128]{2,1,0:T(8,128)(2,1)}, u32[]{:S(2)}, u32[]{:S(2)}) %collective-permute-start.2) | collective-permute-done | bytes 131104 | tf_op jit(solution)/shard_map/ppermute | solution.py:13
  186.5 1.4 copy.166
  187.8 1.4 convolution_bitcast_fusion.3
  189.2 5.2 %collective-permute-done.3 = bf16[16,32,128]{2,1,0:T(8,128)(2,1)S(1)} collective-permute-done((bf16[16,32,128]{2,1,0:T(8,128)(2,1)}, bf16[16,32,128]{2,1,0:T(8,128)(2,1)S(1)}, u32[]{:S(2)}, u32[]{:S(2)}) %collective-permute-start.3) | collective-permute-done | bytes 131104 | tf_op jit(solution)/shard_map/ppermute | solution.py:13
  194.4 0.4 copy.164
  194.9 1.5 convolution_bitcast_fusion.4
  196.3 7.1 %collective-permute-done.4 = bf16[16,32,128]{2,1,0:T(8,128)(2,1)} collective-permute-done((bf16[16,32,128]{2,1,0:T(8,128)(2,1)S(1)}, bf16[16,32,128]{2,1,0:T(8,128)(2,1)}, u32[]{:S(2)}, u32[]{:S(2)}) %collective-permute-start.4) | collective-permute-done | bytes 131104 | tf_op jit(solution)/shard_map/ppermute | solution.py:13
  203.4 1.4 copy.162
  204.8 1.4 convolution_bitcast_fusion.5
  206.2 5.1 %collective-permute-done.5 = bf16[16,32,128]{2,1,0:T(8,128)(2,1)S(1)} collective-permute-done((bf16[16,32,128]{2,1,0:T(8,128)(2,1)}, bf16[16,32,128]{2,1,0:T(8,128)(2,1)S(1)}, u32[]{:S(2)}, u32[]{:S(2)}) %collective-permute-start.5) | collective-permute-done | bytes 131104 | tf_op jit(solution)/shard_map/ppermute | solution.py:13
  211.3 0.4 copy.160
  211.7 1.4 convolution_bitcast_fusion.6
  213.1 6.0 %collective-permute-done.6 = bf16[16,32,128]{2,1,0:T(8,128)(2,1)} collective-permute-done((bf16[16,32,128]{2,1,0:T(8,128)(2,1)S(1)}, bf16[16,32,128]{2,1,0:T(8,128)(2,1)}, u32[]{:S(2)}, u32[]{:S(2)}) %collective-permute-start.6) | collective-permute-done | bytes 131104 | tf_op jit(solution)/shard_map/ppermute | solution.py:13
  219.1 1.3 copy.158
  220.4 1.4 convolution_bitcast_fusion.7
  221.8 13.1 %concatenate.13 = f32[256,16,128]{0,1,2:T(8,128)} concatenate(f32[16,16,128]{0,1,2:T(8,128)} %convolution_bitcast_fusion.7, f32[16,16,128]{0,1,2:T(8,128)} %convolution_bitcast_fusion.6, f32[16,16,128]{0,1,2:T(8,128)} %convolution_bitcast_fusion.5, f32[16,16,128]{0,1,2:T(8,128)} %convolution_bitcast_fusion.4, f32[16,16,128]{0,1,2:T(8,128)} %convolution_bitcast_fusion.3, ...), dimensions={0} | concatenate | bytes 4194304 | tf_op jit(solution)/shard_map/jit(_roll_dynamic)/concatenate | solution.py:20
  234.9 1.9 constant_dynamic-slice_fusion
  236.8 1.6 copy.173
  238.5 20.8 %reduce-scatter.2.cloned.1.call-done = f32[32,16,128]{2,1,0:T(8,128)} async-done(((f32[128,16,128]{2,1,0:T(8,128)}), f32[32,16,128]{2,1,0:T(8,128)}) %reduce-scatter.2.cloned.1.call-update) | async-done | bytes 262160 | tf_op jit(solution)/shard_map/reduce_scatter | solution.py:128
  259.3 1.1 bitcast_reduce_fusion
  260.5 1.2 multiply_reduce_fusion.1
  261.9 1.2 multiply_convert_fusion.1
  263.0 1.2 fusion.95
  265.2 0.7 add_convert_fusion
  (71 shorter events, 4.1 us)
Async XLA Ops:
  7.2 14.7 %copy-start = (bf16[1024,4,256]{2,1,0:T(4,128)(2,1)S(1)}, bf16[1024,4,256]{2,1,0:T(4,128)(2,1)}, u32[]{:S(2)}) copy-start(bf16[1024,4,256]{2,1,0:T(4,128)(2,1)} %param.18) | copy-start | bytes 6291460
  9.6 77.8 %copy-start.10 = (f32[32]{0:T(128)S(1)}, f32[32]{0:T(128)}, u32[]{:S(2)}) copy-start(f32[32]{0:T(128)} %param.21) | copy-start | bytes 388
  11.8 75.7 %all-to-all-start = ((f32[4,1,4096]{2,1,0:T(1,128)}), f32[4,1,4096]{2,1,0:T(1,128)S(1)}, u32[]{:S(2)}, u32[]{:S(2)}) async-start(f32[4,1,4096]{2,1,0:T(1,128)} %reshape.259), calls=%async_computation | async-start | bytes 131072 | tf_op jit(solution)/shard_map/all_to_all | solution.py:56
  16.0 110.2 %all-reduce.2.cloned.1.call-start = ((), (), s32[]{:S(2)}) async-start(), calls=%async_computation.2 | async-start | bytes 131072 | tf_op jit(solution)/shard_map/psum | solution.py:95
  21.9 69.8 %copy-start.4 = (bf16[256,1024]{1,0:T(8,128)(2,1)S(1)}, bf16[256,1024]{1,0:T(8,128)(2,1)}, u32[]{:S(2)}) copy-start(bf16[256,1024]{1,0:T(8,128)(2,1)} %param.19) | copy-start | bytes 1572868
  23.7 70.2 %copy-start.5 = (bf16[128,5,128]{2,0,1:T(8,128)(2,1)S(1)}, bf16[128,5,128]{2,0,1:T(8,128)(2,1)}, u32[]{:S(2)}) copy-start(bf16[128,5,128]{2,0,1:T(8,128)(2,1)} %param.24) | copy-start | bytes 491524
  23.7 102.5 %copy-start.3 = (bf16[16,1024]{1,0:T(8,128)(2,1)S(1)}, bf16[16,1024]{1,0:T(8,128)(2,1)}, u32[]{:S(2)}) copy-start(bf16[16,1024]{1,0:T(8,128)(2,1)} %param.14) | copy-start | bytes 98308
  88.0 71.4 %copy-start.2 = (bf16[16,32,128]{2,1,0:T(8,128)(2,1)S(1)}, bf16[16,32,128]{2,1,0:T(8,128)(2,1)}, u32[]{:S(2)}) copy-start(bf16[16,32,128]{2,1,0:T(8,128)(2,1)} %param.15) | copy-start | bytes 393220
  93.2 166.1 %reduce-scatter.2.cloned.1.call-start = ((), (), s32[]{:S(2)}) async-start(), calls=%async_computation.3 | async-start | bytes 1310720 | tf_op jit(solution)/shard_map/reduce_scatter | solution.py:128
  127.2 32.1 %copy-start.6 = (bf16[16,1024]{1,0:T(8,128)(2,1)}, bf16[16,1024]{1,0:T(8,128)(2,1)S(1)}, u32[]{:S(2)}) copy-start(bf16[16,1024]{1,0:T(8,128)(2,1)S(1)} %get-tuple-element.3) | copy-start | bytes 98308
  161.2 1.1 copy-start.1
  163.0 7.8 %collective-permute-start = (bf16[16,32,128]{2,1,0:T(8,128)(2,1)S(1)}, bf16[16,32,128]{2,1,0:T(8,128)(2,1)}, u32[]{:S(2)}, u32[]{:S(2)}) collective-permute-start(bf16[16,32,128]{2,1,0:T(8,128)(2,1)S(1)} %get-tuple-element.4), channel_id=1, source_target_pairs={{0,4},{4,8},{8,12},{12,16},{16,20},{20,24},{24,28},{28,0},{1,5},{5... | collective-permute-start | bytes 393224 | tf_op jit(solution)/shard_map/ppermute | solution.py:13
  170.8 7.9 %collective-permute-start.1 = (bf16[16,32,128]{2,1,0:T(8,128)(2,1)}, bf16[16,32,128]{2,1,0:T(8,128)(2,1)S(1)}, u32[]{:S(2)}, u32[]{:S(2)}) collective-permute-start(bf16[16,32,128]{2,1,0:T(8,128)(2,1)} %collective-permute-done), channel_id=1, source_target_pairs={{0,4},{4,8},{8,12},{12,16},{16,20},{20,24},{24,28},{28,0},{1,5},{5... | collective-permute-start | bytes 393224 | tf_op jit(solution)/shard_map/ppermute | solution.py:13
  178.7 7.8 %collective-permute-start.2 = (bf16[16,32,128]{2,1,0:T(8,128)(2,1)S(1)}, bf16[16,32,128]{2,1,0:T(8,128)(2,1)}, u32[]{:S(2)}, u32[]{:S(2)}) collective-permute-start(bf16[16,32,128]{2,1,0:T(8,128)(2,1)S(1)} %collective-permute-done.1), channel_id=1, source_target_pairs={{0,4},{4,8},{8,12},{12,16},{16,20},{20,24},{24,28},{28,0},{1,5},{5... | collective-permute-start | bytes 393224 | tf_op jit(solution)/shard_map/ppermute | solution.py:13
  186.5 8.0 %collective-permute-start.3 = (bf16[16,32,128]{2,1,0:T(8,128)(2,1)}, bf16[16,32,128]{2,1,0:T(8,128)(2,1)S(1)}, u32[]{:S(2)}, u32[]{:S(2)}) collective-permute-start(bf16[16,32,128]{2,1,0:T(8,128)(2,1)} %collective-permute-done.2), channel_id=1, source_target_pairs={{0,4},{4,8},{8,12},{12,16},{16,20},{20,24},{24,28},{28,0},{1,5},{5... | collective-permute-start | bytes 393224 | tf_op jit(solution)/shard_map/ppermute | solution.py:13
  194.4 9.0 %collective-permute-start.4 = (bf16[16,32,128]{2,1,0:T(8,128)(2,1)S(1)}, bf16[16,32,128]{2,1,0:T(8,128)(2,1)}, u32[]{:S(2)}, u32[]{:S(2)}) collective-permute-start(bf16[16,32,128]{2,1,0:T(8,128)(2,1)S(1)} %collective-permute-done.3), channel_id=1, source_target_pairs={{0,4},{4,8},{8,12},{12,16},{16,20},{20,24},{24,28},{28,0},{1,5},{5... | collective-permute-start | bytes 393224 | tf_op jit(solution)/shard_map/ppermute | solution.py:13
  203.4 7.9 %collective-permute-start.5 = (bf16[16,32,128]{2,1,0:T(8,128)(2,1)}, bf16[16,32,128]{2,1,0:T(8,128)(2,1)S(1)}, u32[]{:S(2)}, u32[]{:S(2)}) collective-permute-start(bf16[16,32,128]{2,1,0:T(8,128)(2,1)} %collective-permute-done.4), channel_id=1, source_target_pairs={{0,4},{4,8},{8,12},{12,16},{16,20},{20,24},{24,28},{28,0},{1,5},{5... | collective-permute-start | bytes 393224 | tf_op jit(solution)/shard_map/ppermute | solution.py:13
  211.3 7.8 %collective-permute-start.6 = (bf16[16,32,128]{2,1,0:T(8,128)(2,1)S(1)}, bf16[16,32,128]{2,1,0:T(8,128)(2,1)}, u32[]{:S(2)}, u32[]{:S(2)}) collective-permute-start(bf16[16,32,128]{2,1,0:T(8,128)(2,1)S(1)} %collective-permute-done.5), channel_id=1, source_target_pairs={{0,4},{4,8},{8,12},{12,16},{16,20},{20,24},{24,28},{28,0},{1,5},{5... | collective-permute-start | bytes 393224 | tf_op jit(solution)/shard_map/ppermute | solution.py:13
  236.8 26.2 %copy-start.9 = (bf16[128,128]{1,0:T(8,128)(2,1)S(1)}, bf16[128,128]{1,0:T(8,128)(2,1)}, u32[]{:S(2)}) copy-start(bf16[128,128]{1,0:T(8,128)(2,1)} %param.25) | copy-start | bytes 98308
  238.4 26.3 %copy-start.7 = (bf16[512,128]{1,0:T(8,128)(2,1)S(1)}, bf16[512,128]{1,0:T(8,128)(2,1)}, u32[]{:S(2)}) copy-start(bf16[512,128]{1,0:T(8,128)(2,1)} %param.27) | copy-start | bytes 393220
  238.4 26.4 %copy-start.8 = (bf16[128,512]{1,0:T(8,128)(2,1)S(1)}, bf16[128,512]{1,0:T(8,128)(2,1)}, u32[]{:S(2)}) copy-start(bf16[128,512]{1,0:T(8,128)(2,1)} %param.26) | copy-start | bytes 393220
Sparse Core Ops, SparseCore 0:
  93.3 32.8 all-reduce.1
  238.6 20.6 reduce-scatter.1
